TPU v7x, 32 devices: a whole 2x2x4 slice. The times are simulated.
32 devices in a mesh: gx: 16 (over z, x, core), gy: 2 (over y).
Axes of the slice: x: 2, y: 2, z: 4, core: 2. Of those that a mesh axis runs over, the one named last changes fastest.
Arguments:
- particles: float32 [64, 2, 64, 1024], P(None, None, 'gx', 'gy'), may hold values from -32 to 32, as said below
- background: float32 [2, 64, 1024], P(None, 'gx', 'gy'), may hold values from -6 to 6
- obs_tile: int32 [16, 256], P('gx', 'gy'), may hold values from 0 to 127
- obs_mask: int32 [16, 16, 256], P(None, 'gx', 'gy'), may hold values 0 or 1
- obs_value: float32 [16, 256], P('gx', 'gy'), may hold values from -6 to 6
- obs_var: float32 [16, 256], P('gx', 'gy'), may hold values from 0.1 to 1
Outputs:
- analysis: float32 [64, 2, 64, 1024], P(None, None, 'gx', 'gy')
Inputs may be any that keep to these rules, and one draw needn't show every extreme that they name: `particles`: each particle is a field of order one to a few. `obs_tile`: an observation's value names tile row t // 128 and tile column t % (128) of its slab.
All inputs are finite; a program needn't handle non-finite values. No bound on the sum of `obs_mask` on one device may be relied on, other than what follows from the above.
Results may differ from a plain program's by a relative error of at most 0.0001.
Values sent between devices are 32-bit elements; how exact they have to be, the bound alone decides.
A program may use at most 64 MiB of HBM per device.

v0:
```python
import jax
import jax.numpy as jnp
from jax import lax
from jax.sharding import PartitionSpec as P

STEPS = 2
TILE = 4
lap_weight = 0.25
prior_weight = 0.05
couple_weight = 0.5
step_length = 1.0
epsilon = 1e-06
highest = lax.Precision.HIGHEST


def with_halo(block, sides, width):
    for axis, dim in sides:
        count = lax.axis_size(axis)
        forward = [(i, i + 1) for i in range(count - 1)]
        forward.append((count - 1, 0))
        backward = [(target, source) for source, target in forward]
        low = lax.ppermute(
            lax.slice_in_dim(block, block.shape[dim] - width, None, axis=dim), axis, forward
        )
        high = lax.ppermute(lax.slice_in_dim(block, 0, width, axis=dim), axis, backward)
        block = jnp.concatenate([low, block, high], axis=dim)
    return block


def laplace_inner(field):
    total = field[..., 1:-1, 2:] + field[..., 1:-1, :-2]
    total = total + field[..., 2:, 1:-1] + field[..., :-2, 1:-1]
    return total - 4.0 * field[..., 1:-1, 1:-1]


def prior_term(deviation):
    padded = with_halo(deviation, (("gx", 2), ("gy", 3)), 2)
    smooth = padded[..., 1:-1, 1:-1] - lap_weight * laplace_inner(padded)
    curved = smooth[..., 1:-1, 1:-1] - lap_weight * laplace_inner(smooth)
    return -prior_weight * (curved + couple_weight * (deviation - deviation[:, ::-1]))


def observe_term(state, table, weights, values, variance):
    count, rows, cols = (state.shape[0], state.shape[2], state.shape[3])
    tile_rows, tile_cols = (rows // TILE, cols // TILE)
    upper = state[:, 0].reshape(count, tile_rows, TILE, tile_cols, TILE)
    cells = upper.transpose(2, 4, 0, 1, 3).reshape(TILE * TILE, count, tile_rows * tile_cols)
    picked = jnp.einsum("cpt,ot->cpo", cells, table, precision=highest)
    mapped = 0.25 * jnp.sum(weights[:, None, :] * picked, axis=0)
    innovation = (values[None, :] - mapped) / variance[None, :]
    contrib = (0.25 * weights)[:, None, :] * innovation[None]
    spread = jnp.einsum("cpo,ot->cpt", contrib, table, precision=highest)
    back = spread.reshape(TILE, TILE, count, tile_rows, tile_cols).transpose(2, 3, 0, 4, 1)
    back = back.reshape(count, rows, cols)
    return jnp.stack([back, jnp.zeros_like(back)], axis=1)


def norm_scale(drift, denominator):
    total = lax.psum(jnp.sum(drift * drift), ("gx", "gy"))
    return step_length / jnp.sqrt(total / denominator + epsilon)


def per_device(particles, background, obs_tile, obs_mask, obs_value, obs_var):
    count = particles.shape[0]
    tiles = particles.shape[2] // TILE * (particles.shape[3] // TILE)
    table = (obs_tile[0][:, None] == jnp.arange(tiles, dtype=jnp.int32)[None, :]).astype(
        jnp.float32
    )
    weights = obs_mask[:, 0, :].astype(jnp.float32)
    values = obs_value[0]
    variance = obs_var[0]
    local_size = particles[0].size
    total_size = float(local_size * lax.axis_size("gx") * lax.axis_size("gy"))
    pair_count = float(count * (count - 1))
    off_diag = 1.0 - jnp.eye(count, dtype=jnp.float32)
    state = particles
    gram = None
    for step in range(STEPS):
        deviation = state - background[None]
        flat_dev = deviation.reshape(count, -1)
        if gram is None:
            gram = lax.psum(jnp.dot(flat_dev, flat_dev.T, precision=highest), ("gx", "gy"))
        gradient = prior_term(deviation) + observe_term(state, table, weights, values, variance)
        flat_grad = gradient.reshape(count, -1)
        diagonal = jnp.diagonal(gram)
        distance = diagonal[:, None] + diagonal[None, :] - 2.0 * gram
        width = jnp.sum(distance * off_diag) / (pair_count * total_size) + epsilon
        kernel = jnp.exp(-distance / (2.0 * width * total_size))
        attract = jnp.dot(kernel, flat_grad, precision=highest)
        pulled = jnp.dot(kernel, flat_dev, precision=highest)
        drift = (attract + (jnp.sum(kernel, axis=1)[:, None] * flat_dev - pulled) / width) / count
        if step + 1 < STEPS:
            cross, square = lax.psum(
                (
                    jnp.dot(flat_dev, drift.T, precision=highest),
                    jnp.dot(drift, drift.T, precision=highest),
                ),
                ("gx", "gy"),
            )
            scale = step_length / jnp.sqrt(jnp.trace(square) / (count * total_size) + epsilon)
            gram = gram + scale * (cross + cross.T) + scale * scale * square
        else:
            scale = norm_scale(drift, count * total_size)
        state = state + scale * drift.reshape(state.shape)
    return state


def solution(mesh):
    return jax.shard_map(
        per_device,
        mesh=mesh,
        in_specs=(
            P(None, None, "gx", "gy"),
            P(None, "gx", "gy"),
            P("gx", "gy"),
            P(None, "gx", "gy"),
            P("gx", "gy"),
            P("gx", "gy"),
        ),
        out_specs=P(None, None, "gx", "gy"),
        check_vma=False,
    )
```

profile of v0, /device:TPU:14, one launch (start us, length us, event | category | flops | bytes accessed | tf_op | source)
XLA Modules:
  0.0 223.9 jit_solution(16743643375088304163)
XLA Ops:
  0.0 2.8 %copy.40 = f32[64,2,4,512]{0,3,2,1:T(8,128)} copy(f32[64,2,4,512]{3,2,1,0:T(4,128)} %param.6) | data formatting | bytes 2097152 | tf_op args[0]
  2.8 2.2 broadcast_subtract_fusion.1
  5.0 1.1 fusion.58
  6.1 2.4 %copy.32 = f32[64,2,2,512]{3,0,2,1:T(8,128)} copy(f32[64,2,2,512]{0,3,2,1:T(8,128)} %get-tuple-element.15) | data formatting | bytes 1048576 | tf_op jit(solution)/shard_map/slice | solution.py:23
  8.5 1.1 copy.33
  9.6 1.7 collective-permute-start.1
  11.3 1.9 slice.112
  13.2 3.6 %convolution_bitcast_fusion.1 = f32[64,64]{1,0:T(8,128)S(1)} fusion(f32[64,2,4,512]{0,3,2,1:T(8,128)S(1)} %broadcast_subtract_fusion.1), kind=kOutput, calls=%fused_computation.61 | convolution fusion | flops 201326592 | bytes 1064960 | tf_op jit(solution)/shard_map/dot_general | solution.py:82
  16.8 1.4 copy.36
  18.2 1.1 copy.37
  19.3 41.9 %psum.28 = f32[64,64]{1,0:T(8,128)S(1)} all-reduce(f32[64,64]{1,0:T(8,128)S(1)} %convolution_bitcast_fusion.1), channel_id=1, replica_groups=mesh['gx'=16,'gy'=2] {'gx','gy'}, use_global_device_ids=true, to_apply=%region_0.0 | all-reduce | flops 4096 | bytes 32768 | tf_op jit(solution)/shard_map/psum | solution.py:82
  61.2 0.8 gather_fusion
  62.1 0.7 multiply_reduce_fusion.2
  63.4 0.2 fusion.55
  63.6 0.6 copy.57
  64.2 1.5 fusion.26
  65.7 3.4 %fusion.1 = f32[64,4096]{1,0:T(8,128)} fusion(f32[64,4096]{0,1:T(8,128)S(1)} %bitcast.63, f32[64,4096]{1,0:T(8,128)S(1)} %copy.57, f32[]{:T(128)S(6)} %add.128, f32[64]{0:T(128)S(1)} %fusion.55, f32[64,64]{1,0:T(8,128)S(1)} %psum.28, f32[]{:T(128)S(6)} %mul.175, f32[64]{0:T(128)S(1)} %gather_fusion), kind=kOutput, calls=%fused_computation.6 | convolution fusion | flops 202133504 | bytes 3162632 | tf_op jit(solution)/shard_map/dot_general | solution.py:90
  69.2 1.4 copy.34
  70.5 2.4 %copy.35 = f32[64,2,2,512]{0,3,2,1:T(8,128)} copy(f32[64,2,2,512]{3,0,2,1:T(8,128)} %collective-permute-done.1) | data formatting | bytes 1048576 | tf_op jit(solution)/shard_map/ppermute | solution.py:25
  72.9 0.8 pad_maximum_fusion.19
  73.7 0.2 collective-permute-start.2
  73.8 1.9 collective-permute-start.3
  75.8 1.2 fusion.35
  77.0 2.4 %copy.38 = f32[4,4,64,1,128]{2,1,4,0,3:T(4,128)} copy(f32[4,4,64,1,128]{4,2,1,0,3:T(8,128)} %bitcast.78) | data formatting | bytes 1048576 | tf_op jit(solution)/shard_map/reshape | solution.py:53
  79.4 1.8 pad_maximum_fusion
  81.1 2.2 %fusion.8 = f32[64,2,6,514]{0,3,2,1:T(8,128)S(1)} fusion(f32[64,2,8,516]{0,3,2,1:T(8,128)S(1)} %pad_maximum_fusion, f32[64,2,8,2]{0,3,2,1:T(2,128)S(1)} %collective-permute-done.2, f32[64,2,2,512]{0,3,2,1:T(8,128)S(1)} %copy-done.1, f32[64,2,4,512]{0,3,2,1:T(8,128)S(1)} %broadcast_subtract_fusion.1, f32[64,2,2,512]{0,3,2,1:T(8,128)S(1)} %copy.34, ...), kind=kLoop, calls=%fused_computation.25 | loop fusion | flops 5131776 | bytes 8429568 | tf_op jit(solution)/shard_map/sub | solution.py:38
  83.4 1.2 fusion.13
  84.6 2.4 %convolution_add_fusion.1 = f32[64,4096]{1,0:T(8,128)S(1)} fusion(f32[64,4096]{1,0:T(8,128)S(1)} %copy-done.3, f32[64,4096]{0,1:T(8,128)S(1)} %bitcast.67, f32[64,64]{1,0:T(8,128)S(1)} %psum.28, f32[]{:T(128)S(6)} %mul.175, f32[64]{0:T(128)S(1)} %gather_fusion), kind=kOutput, calls=%fused_computation.7 | convolution fusion | flops 201609216 | bytes 3162372 | tf_op jit(solution)/shard_map/dot_general | solution.py:89
  87.1 1.5 fusion.27
  88.6 1.0 fusion.29
  89.6 39.4 %all-reduce.2 = (f32[64,64]{1,0:T(8,128)S(1)}, f32[64,64]{0,1:T(8,128)S(1)}) all-reduce(f32[64,64]{1,0:T(8,128)S(1)} %fusion.29, f32[64,64]{0,1:T(8,128)S(1)} %fusion.27), channel_id=1, replica_groups=mesh['gx'=16,'gy'=2] {'gx','gy'}, use_global_device_ids=true, to_apply=%region_4.5 | all-reduce | flops 8192 | bytes 65536 | tf_op jit(solution)/shard_map/psum | solution.py:93
  129.0 0.6 select_reduce_fusion
  130.3 0.1 broadcast_multiply_fusion.1
  130.4 1.9 copy.58
  132.3 3.5 %broadcast_subtract_fusion = (f32[64,2,4,512]{0,3,2,1:T(8,128)S(1)}, f32[64,2,4,512]{0,3,2,1:T(8,128)}) fusion(f32[2,4,512]{2,1,0:T(4,128)S(1)} %copy-done.7, f32[64,2,4,512]{0,3,2,1:T(8,128)} %copy.40, f32[64,2,4,512]{0,3,2,1:T(8,128)} %bitcast.70), kind=kLoop, calls=%fused_computation.63 | loop fusion | flops 524288 | bytes 4210688 | tf_op jit(solution)/shard_map/sub | solution.py:79
  135.8 1.1 fusion.57
  136.9 2.4 %copy.44 = f32[64,2,2,512]{3,0,2,1:T(8,128)} copy(f32[64,2,2,512]{0,3,2,1:T(8,128)} %get-tuple-element.13) | data formatting | bytes 1048576 | tf_op jit(solution)/shard_map/slice | solution.py:23
  139.3 1.1 copy.45
  140.4 1.7 collective-permute-start.5
  142.1 1.3 slice.152
  143.4 1.1 copy.48
  144.5 1.5 fusion.25
  146.1 0.8 gather_fusion.1
  147.0 0.7 multiply_reduce_fusion.1
  148.3 0.2 fusion.56
  148.5 0.6 copy.59
  149.1 3.4 %fusion = f32[64,4096]{1,0:T(8,128)} fusion(f32[64,4096]{0,1:T(8,128)S(1)} %bitcast.66, f32[64,4096]{1,0:T(8,128)S(1)} %copy.59, f32[]{:T(128)S(6)} %add.146, f32[64]{0:T(128)S(1)} %fusion.56, f32[64,64]{1,0:T(8,128)S(1)} %fusion.48, f32[]{:T(128)S(6)} %mul.204, f32[64]{0:T(128)S(1)} %gather_fusion.1), kind=kOutput, calls=%fused_computation.3 | convolution fusion | flops 202133504 | bytes 3162632 | tf_op jit(solution)/shard_map/dot_general | solution.py:90
  152.5 1.3 collective-permute-done.4
  153.8 1.4 copy.46
  155.2 2.4 %copy.47 = f32[64,2,2,512]{0,3,2,1:T(8,128)} copy(f32[64,2,2,512]{3,0,2,1:T(8,128)} %collective-permute-done.5) | data formatting | bytes 1048576 | tf_op jit(solution)/shard_map/ppermute | solution.py:25
  157.5 0.8 pad_maximum_fusion.16
  158.3 1.3 collective-permute-start.6
  159.6 0.8 collective-permute-start.7
  160.4 1.2 fusion.31
  161.6 2.4 %copy.49 = f32[4,4,64,1,128]{2,1,4,0,3:T(4,128)} copy(f32[4,4,64,1,128]{4,2,1,0,3:T(8,128)} %bitcast.77) | data formatting | bytes 1048576 | tf_op jit(solution)/shard_map/reshape | solution.py:53
  164.0 1.7 pad_maximum_fusion.1
  165.8 2.2 %fusion.4 = f32[64,2,6,514]{0,3,2,1:T(8,128)S(1)} fusion(f32[64,2,8,516]{0,3,2,1:T(8,128)S(1)} %pad_maximum_fusion.1, f32[64,2,8,2]{0,3,2,1:T(2,128)S(1)} %collective-permute-done.6, f32[64,2,2,512]{0,3,2,1:T(8,128)S(1)} %copy-done, f32[64,2,4,512]{0,3,2,1:T(8,128)S(1)} %get-tuple-element.7, f32[64,2,2,512]{0,3,2,1:T(8,128)S(1)} %copy.46, ...), kind=kLoop, calls=%fused_computation.13 | loop fusion | flops 5131776 | bytes 8429568 | tf_op jit(solution)/shard_map/sub | solution.py:38
  168.0 1.2 fusion.17
  169.3 3.1 %multiply_reduce_fusion = (f32[]{:T(128)}, f32[64,4096]{1,0:T(8,128)S(1)}) fusion(f32[64,4096]{1,0:T(8,128)S(1)} %copy-done.4, f32[64,4096]{0,1:T(8,128)S(1)} %bitcast.69, f32[64,64]{1,0:T(8,128)S(1)} %fusion.48, f32[]{:T(128)S(6)} %mul.204, f32[64]{0:T(128)S(1)} %gather_fusion.1), kind=kOutput, calls=%fused_computation.62 | convolution fusion | flops 202395648 | bytes 3162376 | tf_op jit(solution)/shard_map/dot_general | solution.py:89
  172.3 43.0 %psum.31 = f32[]{:T(128)} all-reduce(f32[]{:T(128)} %get-tuple-element.17), channel_id=1, replica_groups=mesh['gx'=16,'gy'=2] {'gx','gy'}, use_global_device_ids=true, to_apply=%region_11.12 | all-reduce | flops 1 | bytes 8 | tf_op jit(solution)/shard_map/psum | solution.py:59
  216.1 0.1 broadcast_multiply_fusion
  216.2 1.9 copy.60
  218.1 3.2 %add.157 = f32[64,2,4,512]{0,3,2,1:T(8,128)} add(f32[64,2,4,512]{0,3,2,1:T(8,128)S(1)} %copy-done.2, f32[64,2,4,512]{0,3,2,1:T(8,128)} %bitcast.68) | non-fusion elementwise | flops 262144 | bytes 3145728 | tf_op jit(solution)/shard_map/add | solution.py:104
  221.2 2.7 %copy.52 = f32[64,2,4,512]{3,2,1,0:T(4,128)} copy(f32[64,2,4,512]{0,3,2,1:T(8,128)} %add.157) | data formatting | bytes 2097152 | tf_op jit(solution)/shard_map/add | solution.py:104
  (40 shorter events, 0.3 us)
Async XLA Ops:
  0.0 2.8 %copy-start.7 = (f32[2,4,512]{2,1,0:T(4,128)S(1)}, f32[2,4,512]{2,1,0:T(4,128)}, u32[]{:S(2)}) copy-start(f32[2,4,512]{2,1,0:T(4,128)} %param.7) | copy-start | bytes 49156
  8.5 60.7 %collective-permute-start = (f32[64,2,2,512]{3,0,2,1:T(8,128)}, f32[64,2,2,512]{3,0,2,1:T(8,128)}, u32[]{:S(2)}, u32[]{:S(2)}) collective-permute-start(f32[64,2,2,512]{3,0,2,1:T(8,128)} %copy.32), channel_id=1, source_target_pairs={{0,2},{2,4},{4,6},{6,8},{8,10},{10,12},{12,14},{14,16},{16,18},{18... | collective-permute-start | bytes 1572872 | tf_op jit(solution)/shard_map/ppermute | solution.py:22
  9.6 60.9 %collective-permute-start.1 = (f32[64,2,2,512]{3,0,2,1:T(8,128)}, f32[64,2,2,512]{3,0,2,1:T(8,128)}, u32[]{:S(2)}, u32[]{:S(2)}) collective-permute-start(f32[64,2,2,512]{3,0,2,1:T(8,128)} %copy.33), channel_id=1, source_target_pairs={{2,0},{4,2},{6,4},{8,6},{10,8},{12,10},{14,12},{16,14},{18,16},{20... | collective-permute-start | bytes 1572872 | tf_op jit(solution)/shard_map/ppermute | solution.py:25
  13.2 3.6 %copy-start.8 = (s32[16,1,128]{2,1,0:T(1,128)S(1)}, s32[16,1,128]{2,1,0:T(1,128)}, u32[]{:S(2)}) copy-start(s32[16,1,128]{2,1,0:T(1,128)} %param.9) | copy-start | bytes 24580
  19.3 44.8 %copy-start.9 = (s32[1,128]{1,0:T(1,128)S(1)}, s32[1,128]{1,0:T(1,128)}, u32[]{:S(2)}) copy-start(s32[1,128]{1,0:T(1,128)} %param.8) | copy-start | bytes 1540
  61.2 4.5 %copy-start.10 = (f32[1,128]{1,0:T(1,128)S(1)}, f32[1,128]{1,0:T(1,128)}, u32[]{:S(2)}) copy-start(f32[1,128]{1,0:T(1,128)} %param.11) | copy-start | bytes 1540
  61.2 4.4 %copy-start.11 = (f32[1,128]{1,0:T(1,128)S(1)}, f32[1,128]{1,0:T(1,128)}, u32[]{:S(2)}) copy-start(f32[1,128]{1,0:T(1,128)} %param.10) | copy-start | bytes 1540
  73.7 5.7 %collective-permute-start.2 = (f32[64,2,8,2]{0,3,2,1:T(2,128)S(1)}, f32[64,2,8,2]{0,3,2,1:T(2,128)S(1)}, u32[]{:S(2)}, u32[]{:S(2)}) collective-permute-start(f32[64,2,8,2]{0,3,2,1:T(2,128)S(1)} %get-tuple-element.11), channel_id=1, source_target_pairs={{0,1},{1,0},{2,3},{3,2},{4,5},{5,4},{6,7},{7,6},{8,9},{9,8},{10,11... | collective-permute-start | bytes 24584 | tf_op jit(solution)/shard_map/ppermute | solution.py:22
  73.8 5.5 %collective-permute-start.3 = (f32[64,2,8,2]{0,3,2,1:T(2,128)S(1)}, f32[64,2,8,2]{0,3,2,1:T(2,128)S(1)}, u32[]{:S(2)}, u32[]{:S(2)}) collective-permute-start(f32[64,2,8,2]{0,3,2,1:T(2,128)S(1)} %get-tuple-element.12), channel_id=1, source_target_pairs={{1,0},{0,1},{3,2},{2,3},{5,4},{4,5},{7,6},{6,7},{9,8},{8,9},{11,10... | collective-permute-start | bytes 24584 | tf_op jit(solution)/shard_map/ppermute | solution.py:25
  79.3 1.8 copy-start.1
  81.1 2.3 %copy-start.6 = (f32[4,4,64,1,128]{2,1,4,0,3:T(4,128)S(1)}, f32[4,4,64,1,128]{2,1,4,0,3:T(4,128)}, u32[]{:S(2)}) copy-start(f32[4,4,64,1,128]{2,1,4,0,3:T(4,128)} %copy.38) | copy-start | bytes 1572868
  83.4 1.2 copy-start.3
  139.3 14.5 %collective-permute-start.4 = (f32[64,2,2,512]{3,0,2,1:T(8,128)}, f32[64,2,2,512]{3,0,2,1:T(8,128)}, u32[]{:S(2)}, u32[]{:S(2)}) collective-permute-start(f32[64,2,2,512]{3,0,2,1:T(8,128)} %copy.44), channel_id=1, source_target_pairs={{0,2},{2,4},{4,6},{6,8},{8,10},{10,12},{12,14},{14,16},{16,18},{18... | collective-permute-start | bytes 1572872 | tf_op jit(solution)/shard_map/ppermute | solution.py:22
  140.4 14.8 %collective-permute-start.5 = (f32[64,2,2,512]{3,0,2,1:T(8,128)}, f32[64,2,2,512]{3,0,2,1:T(8,128)}, u32[]{:S(2)}, u32[]{:S(2)}) collective-permute-start(f32[64,2,2,512]{3,0,2,1:T(8,128)} %copy.45), channel_id=1, source_target_pairs={{2,0},{4,2},{6,4},{8,6},{10,8},{12,10},{14,12},{16,14},{18,16},{20... | collective-permute-start | bytes 1572872 | tf_op jit(solution)/shard_map/ppermute | solution.py:25
  158.3 5.7 %collective-permute-start.6 = (f32[64,2,8,2]{0,3,2,1:T(2,128)S(1)}, f32[64,2,8,2]{0,3,2,1:T(2,128)S(1)}, u32[]{:S(2)}, u32[]{:S(2)}) collective-permute-start(f32[64,2,8,2]{0,3,2,1:T(2,128)S(1)} %get-tuple-element.9), channel_id=1, source_target_pairs={{0,1},{1,0},{2,3},{3,2},{4,5},{5,4},{6,7},{7,6},{8,9},{9,8},{10,11... | collective-permute-start | bytes 24584 | tf_op jit(solution)/shard_map/ppermute | solution.py:22
  159.6 4.4 %collective-permute-start.7 = (f32[64,2,8,2]{0,3,2,1:T(2,128)S(1)}, f32[64,2,8,2]{0,3,2,1:T(2,128)S(1)}, u32[]{:S(2)}, u32[]{:S(2)}) collective-permute-start(f32[64,2,8,2]{0,3,2,1:T(2,128)S(1)} %get-tuple-element.10), channel_id=1, source_target_pairs={{1,0},{0,1},{3,2},{2,3},{5,4},{4,5},{7,6},{6,7},{9,8},{8,9},{11,10... | collective-permute-start | bytes 24584 | tf_op jit(solution)/shard_map/ppermute | solution.py:25
  164.0 1.8 copy-start
  165.8 2.3 %copy-start.5 = (f32[4,4,64,1,128]{2,1,4,0,3:T(4,128)S(1)}, f32[4,4,64,1,128]{2,1,4,0,3:T(4,128)}, u32[]{:S(2)}) copy-start(f32[4,4,64,1,128]{2,1,4,0,3:T(4,128)} %copy.49) | copy-start | bytes 1572868
  168.0 1.2 copy-start.4
  216.1 1.9 copy-start.2
where the time goes:
time: 225 us; the launch traced here: 224 us
  blocking collectives  124 us (55%)
  local copies, waits for them, and re-layouts  40.5 us (18%)
  matrix products  23.9 us (11%)
  other arithmetic  23.2 us (10%)
  starting transfers between devices  7.67 us (3%)
  between operations  3.05 us (1%)
    psum x1, blocking collectives, norm_scale(): total = lax.psum(jnp.sum(drift * drift), ('gx', 'gy'))  43 us
    psum x1, blocking collectives, per_device(): lax.psum(jnp.dot(flat_dev, flat_dev.T, precision=highest), ('gx', 'gy'))  41.9 us
    psum x1, blocking collectives, per_device(): lax.psum((jnp.dot(flat_dev, drift.T, precision=highest), jnp.dot(drift, d...  39.4 us
    slice x4, local copies, waits for them, and re-layouts, with_halo(): lax.slice_in_dim(block, block.shape[dim] - width, None, axis=dim)  6.94 us
    dot_general x2, matrix products, per_device(): pulled = jnp.dot(kernel, flat_dev, precision=highest)  6.85 us
    ppermute x4, starting transfers between devices, with_halo(): lax.ppermute(lax.slice_in_dim(block, 0, width, axis=dim), axis, backward)  6.21 us
    sub x2, other arithmetic, per_device(): deviation = state - background[None]  5.68 us
    dot_general x2, matrix products, per_device(): attract = jnp.dot(kernel, flat_grad, precision=highest)  5.5 us
  transfers between devices with their start and end apart: 8, of which 1 were waited for; matrix products, arithmetic and copies ran while one was open for 17% of the time, Pallas kernels for 0%

commit v1 on v0

--- a/solution.py
+++ b/solution.py
@@ -79,7 +79,10 @@
         deviation = state - background[None]
         flat_dev = deviation.reshape(count, -1)
         if gram is None:
-            gram = lax.psum(jnp.dot(flat_dev, flat_dev.T, precision=highest), ("gx", "gy"))
+            gram = jnp.sum(
+                lax.all_gather(jnp.dot(flat_dev, flat_dev.T, precision=highest), ("gx", "gy")),
+                axis=0,
+            )
         gradient = prior_term(deviation) + observe_term(state, table, weights, values, variance)
         flat_grad = gradient.reshape(count, -1)
         diagonal = jnp.diagonal(gram)

time: 225 us -> 255 us (1.13)
  blocking collectives: 124 us -> 152 us
    all_gather x0 -> x1, blocking collectives: none -> 55 us  [per_device(): lax.all_gather(jnp.dot(flat_dev, flat_dev.T, precision=highest), ('gx', '...]
    psum x1 -> x0, blocking collectives: 41.9 us -> none  [per_device(): lax.psum(jnp.dot(flat_dev, flat_dev.T, precision=highest), ('gx', 'gy'))]
    psum x1, blocking collectives: 39.4 us -> 56.8 us  [per_device(): lax.psum((jnp.dot(flat_dev, drift.T, precision=highest), jnp.dot(drift, d...]
    psum x1, blocking collectives: 43 us -> 40.5 us  [norm_scale(): total = lax.psum(jnp.sum(drift * drift), ('gx', 'gy'))]
  transfers between devices with their start and end apart: 8 -> 8, of which waited for: 1 -> 1; matrix products, arithmetic and copies ran while one was open for 17% -> 15% of each run, Pallas kernels for 0% -> 0%
where the time goes in v1:
time: 255 us; the launch traced here: 252 us
  blocking collectives  152 us (60%)
  local copies, waits for them, and re-layouts  40.5 us (16%)
  matrix products  23.9 us (9%)
  other arithmetic  23.3 us (9%)
  starting transfers between devices  7.67 us (3%)
  between operations  3.05 us (1%)
    psum x1, blocking collectives, per_device(): lax.psum((jnp.dot(flat_dev, drift.T, precision=highest), jnp.dot(drift, d...  56.8 us
    all_gather x1, blocking collectives, per_device(): lax.all_gather(jnp.dot(flat_dev, flat_dev.T, precision=highest), ('gx', '...  55 us
    psum x1, blocking collectives, norm_scale(): total = lax.psum(jnp.sum(drift * drift), ('gx', 'gy'))  40.5 us
    slice x4, local copies, waits for them, and re-layouts, with_halo(): lax.slice_in_dim(block, block.shape[dim] - width, None, axis=dim)  6.92 us
    dot_general x2, matrix products, per_device(): pulled = jnp.dot(kernel, flat_dev, precision=highest)  6.85 us
    sub x2, other arithmetic, per_device(): deviation = state - background[None]  5.68 us
    ppermute x4, starting transfers between devices, with_halo(): lax.ppermute(lax.slice_in_dim(block, 0, width, axis=dim), axis, backward)  5.6 us
    dot_general x2, matrix products, per_device(): attract = jnp.dot(kernel, flat_grad, precision=highest)  5.5 us
  transfers between devices with their start and end apart: 8, of which 1 were waited for; matrix products, arithmetic and copies ran while one was open for 15% of the time, Pallas kernels for 0%

profile of v1, /device:TPU:14, one launch (start us, length us, event | category | flops | bytes accessed | tf_op | source)
XLA Modules:
  0.0 252.0 jit_solution(482518923436061661)
XLA Ops:
  0.0 2.8 %copy.40 = f32[64,2,4,512]{0,3,2,1:T(8,128)} copy(f32[64,2,4,512]{3,2,1,0:T(4,128)} %param.6) | data formatting | bytes 2097152 | tf_op args[0]
  2.8 2.2 broadcast_subtract_fusion.1
  5.0 1.1 fusion.58
  6.1 2.4 copy.32
  8.5 1.1 copy.33
  9.6 1.7 collective-permute-start.1
  11.3 1.9 slice.112
  13.2 3.6 %convolution_bitcast_fusion.1 = f32[64,64]{1,0:T(8,128)S(1)} fusion(f32[64,2,4,512]{0,3,2,1:T(8,128)S(1)} %broadcast_subtract_fusion.1), kind=kOutput, calls=%fused_computation.61 | convolution fusion | flops 201326592 | bytes 1064960 | tf_op jit(solution)/shard_map/dot_general | solution.py:83
  16.8 1.4 copy.36
  18.2 1.1 copy.37
  19.3 55.0 %all-gather = f32[2048,64]{1,0:T(8,128)S(1)} all-gather(f32[64,64]{1,0:T(8,128)S(1)} %convolution_bitcast_fusion.1), channel_id=2, replica_groups=mesh['gx'=16,'gy'=2] {'gx','gy'}, dimensions={0}, use_global_device_ids=true | all-gather | bytes 540672 | tf_op jit(solution)/shard_map/all_gather | solution.py:83
  74.4 0.1 reduce_sum.82
  74.5 0.8 gather_fusion
  75.3 0.7 multiply_reduce_fusion.2
  76.6 0.2 fusion.55
  76.8 0.6 copy.57
  77.4 1.5 fusion.26
  79.0 3.4 %fusion.1 = f32[64,4096]{1,0:T(8,128)} fusion(f32[64,4096]{0,1:T(8,128)S(1)} %bitcast.64, f32[64,4096]{1,0:T(8,128)S(1)} %copy.57, f32[]{:T(128)S(6)} %add.126, f32[64]{0:T(128)S(1)} %fusion.55, f32[64,64]{1,0:T(8,128)S(1)} %reduce_sum.82, f32[]{:T(128)S(6)} %mul.175, f32[64]{0:T(128)S(1)} %gather_fusion), kind=kOutput, calls=%fused_computation.6 | convolution fusion | flops 202133504 | bytes 3162632 | tf_op jit(solution)/shard_map/dot_general | solution.py:93
  82.4 1.4 copy.34
  83.8 2.4 copy.35
  86.2 0.8 pad_maximum_fusion.19
  86.9 0.4 collective-permute-start.2
  87.3 1.7 collective-permute-start.3
  89.0 1.2 fusion.35
  90.2 2.4 copy.38
  92.6 1.8 pad_maximum_fusion
  94.4 2.2 fusion.8
  96.7 1.2 fusion.13
  97.9 2.4 convolution_add_fusion.1
  100.3 1.5 fusion.27
  101.9 1.0 fusion.29
  102.8 56.8 %all-reduce.2 = (f32[64,64]{1,0:T(8,128)S(1)}, f32[64,64]{0,1:T(8,128)S(1)}) all-reduce(f32[64,64]{1,0:T(8,128)S(1)} %fusion.29, f32[64,64]{0,1:T(8,128)S(1)} %fusion.27), channel_id=1, replica_groups=mesh['gx'=16,'gy'=2] {'gx','gy'}, use_global_device_ids=true, to_apply=%region_4.5 | all-reduce | flops 8192 | bytes 65536 | tf_op jit(solution)/shard_map/psum | solution.py:96
  159.6 0.6 select_reduce_fusion
  160.9 0.1 broadcast_multiply_fusion.1
  161.0 1.9 copy.58
  162.9 3.5 %broadcast_subtract_fusion = (f32[64,2,4,512]{0,3,2,1:T(8,128)S(1)}, f32[64,2,4,512]{0,3,2,1:T(8,128)}) fusion(f32[2,4,512]{2,1,0:T(4,128)S(1)} %copy-done.7, f32[64,2,4,512]{0,3,2,1:T(8,128)} %copy.40, f32[64,2,4,512]{0,3,2,1:T(8,128)} %bitcast.71), kind=kLoop, calls=%fused_computation.63 | loop fusion | flops 524288 | bytes 4210688 | tf_op jit(solution)/shard_map/sub | solution.py:79
  166.4 1.1 fusion.57
  167.5 2.4 copy.44
  169.9 1.1 copy.45
  171.0 1.7 collective-permute-start.5
  172.7 1.3 slice.152
  174.0 1.1 copy.48
  175.2 1.5 fusion.25
  176.8 0.8 gather_fusion.1
  177.6 0.7 multiply_reduce_fusion.1
  178.9 0.2 fusion.56
  179.1 0.6 copy.59
  179.7 3.4 %fusion = f32[64,4096]{1,0:T(8,128)} fusion(f32[64,4096]{0,1:T(8,128)S(1)} %bitcast.67, f32[64,4096]{1,0:T(8,128)S(1)} %copy.59, f32[]{:T(128)S(6)} %add.144, f32[64]{0:T(128)S(1)} %fusion.56, f32[64,64]{1,0:T(8,128)S(1)} %fusion.48, f32[]{:T(128)S(6)} %mul.204, f32[64]{0:T(128)S(1)} %gather_fusion.1), kind=kOutput, calls=%fused_computation.3 | convolution fusion | flops 202133504 | bytes 3162632 | tf_op jit(solution)/shard_map/dot_general | solution.py:93
  183.1 1.3 collective-permute-done.4
  184.4 1.4 copy.46
  185.8 2.4 copy.47
  188.2 0.8 pad_maximum_fusion.16
  188.9 1.6 collective-permute-start.6
  190.5 0.5 collective-permute-start.7
  191.0 1.2 fusion.31
  192.2 2.4 copy.49
  194.6 1.7 pad_maximum_fusion.1
  196.4 2.2 fusion.4
  198.7 1.2 fusion.17
  199.9 3.1 %multiply_reduce_fusion = (f32[]{:T(128)}, f32[64,4096]{1,0:T(8,128)S(1)}) fusion(f32[64,4096]{1,0:T(8,128)S(1)} %copy-done.4, f32[64,4096]{0,1:T(8,128)S(1)} %bitcast.70, f32[64,64]{1,0:T(8,128)S(1)} %fusion.48, f32[]{:T(128)S(6)} %mul.204, f32[64]{0:T(128)S(1)} %gather_fusion.1), kind=kOutput, calls=%fused_computation.62 | convolution fusion | flops 202395648 | bytes 3162376 | tf_op jit(solution)/shard_map/dot_general | solution.py:92
  202.9 40.5 %psum.23 = f32[]{:T(128)} all-reduce(f32[]{:T(128)} %get-tuple-element.17), channel_id=1, replica_groups=mesh['gx'=16,'gy'=2] {'gx','gy'}, use_global_device_ids=true, to_apply=%region_11.12 | all-reduce | flops 1 | bytes 8 | tf_op jit(solution)/shard_map/psum | solution.py:59
  244.2 1.9 copy.60
  246.1 3.2 %add.155 = f32[64,2,4,512]{0,3,2,1:T(8,128)} add(f32[64,2,4,512]{0,3,2,1:T(8,128)S(1)} %copy-done.2, f32[64,2,4,512]{0,3,2,1:T(8,128)} %bitcast.69) | non-fusion elementwise | flops 262144 | bytes 3145728 | tf_op jit(solution)/shard_map/add | solution.py:107
  249.3 2.7 %copy.52 = f32[64,2,4,512]{3,2,1,0:T(4,128)} copy(f32[64,2,4,512]{0,3,2,1:T(8,128)} %add.155) | data formatting | bytes 2097152 | tf_op jit(solution)/shard_map/add | solution.py:107
  (41 shorter events, 0.4 us)
Async XLA Ops:
  0.0 2.8 %copy-start.7 = (f32[2,4,512]{2,1,0:T(4,128)S(1)}, f32[2,4,512]{2,1,0:T(4,128)}, u32[]{:S(2)}) copy-start(f32[2,4,512]{2,1,0:T(4,128)} %param.7) | copy-start | bytes 49156
  8.5 73.9 %collective-permute-start = (f32[64,2,2,512]{3,0,2,1:T(8,128)}, f32[64,2,2,512]{3,0,2,1:T(8,128)}, u32[]{:S(2)}, u32[]{:S(2)}) collective-permute-start(f32[64,2,2,512]{3,0,2,1:T(8,128)} %copy.32), channel_id=1, source_target_pairs={{0,2},{2,4},{4,6},{6,8},{8,10},{10,12},{12,14},{14,16},{16,18},{18... | collective-permute-start | bytes 1572872 | tf_op jit(solution)/shard_map/ppermute | solution.py:22
  9.6 74.2 %collective-permute-start.1 = (f32[64,2,2,512]{3,0,2,1:T(8,128)}, f32[64,2,2,512]{3,0,2,1:T(8,128)}, u32[]{:S(2)}, u32[]{:S(2)}) collective-permute-start(f32[64,2,2,512]{3,0,2,1:T(8,128)} %copy.33), channel_id=1, source_target_pairs={{2,0},{4,2},{6,4},{8,6},{10,8},{12,10},{14,12},{16,14},{18,16},{20... | collective-permute-start | bytes 1572872 | tf_op jit(solution)/shard_map/ppermute | solution.py:25
  13.2 3.6 %copy-start.8 = (s32[16,1,128]{2,1,0:T(1,128)S(1)}, s32[16,1,128]{2,1,0:T(1,128)}, u32[]{:S(2)}) copy-start(s32[16,1,128]{2,1,0:T(1,128)} %param.9) | copy-start | bytes 24580
  74.5 2.9 %copy-start.9 = (s32[1,128]{1,0:T(1,128)S(1)}, s32[1,128]{1,0:T(1,128)}, u32[]{:S(2)}) copy-start(s32[1,128]{1,0:T(1,128)} %param.8) | copy-start | bytes 1540
  74.5 4.5 %copy-start.10 = (f32[1,128]{1,0:T(1,128)S(1)}, f32[1,128]{1,0:T(1,128)}, u32[]{:S(2)}) copy-start(f32[1,128]{1,0:T(1,128)} %param.11) | copy-start | bytes 1540
  74.5 4.5 %copy-start.11 = (f32[1,128]{1,0:T(1,128)S(1)}, f32[1,128]{1,0:T(1,128)}, u32[]{:S(2)}) copy-start(f32[1,128]{1,0:T(1,128)} %param.10) | copy-start | bytes 1540
  86.9 5.7 %collective-permute-start.2 = (f32[64,2,8,2]{0,3,2,1:T(2,128)S(1)}, f32[64,2,8,2]{0,3,2,1:T(2,128)S(1)}, u32[]{:S(2)}, u32[]{:S(2)}) collective-permute-start(f32[64,2,8,2]{0,3,2,1:T(2,128)S(1)} %get-tuple-element.11), channel_id=1, source_target_pairs={{0,1},{1,0},{2,3},{3,2},{4,5},{5,4},{6,7},{7,6},{8,9},{9,8},{10,11... | collective-permute-start | bytes 24584 | tf_op jit(solution)/shard_map/ppermute | solution.py:22
  87.3 5.3 %collective-permute-start.3 = (f32[64,2,8,2]{0,3,2,1:T(2,128)S(1)}, f32[64,2,8,2]{0,3,2,1:T(2,128)S(1)}, u32[]{:S(2)}, u32[]{:S(2)}) collective-permute-start(f32[64,2,8,2]{0,3,2,1:T(2,128)S(1)} %get-tuple-element.12), channel_id=1, source_target_pairs={{1,0},{0,1},{3,2},{2,3},{5,4},{4,5},{7,6},{6,7},{9,8},{8,9},{11,10... | collective-permute-start | bytes 24584 | tf_op jit(solution)/shard_map/ppermute | solution.py:25
  92.6 1.8 copy-start.1
  94.4 2.3 copy-start.6
  96.6 1.2 copy-start.3
  169.9 14.5 %collective-permute-start.4 = (f32[64,2,2,512]{3,0,2,1:T(8,128)}, f32[64,2,2,512]{3,0,2,1:T(8,128)}, u32[]{:S(2)}, u32[]{:S(2)}) collective-permute-start(f32[64,2,2,512]{3,0,2,1:T(8,128)} %copy.44), channel_id=1, source_target_pairs={{0,2},{2,4},{4,6},{6,8},{8,10},{10,12},{12,14},{14,16},{16,18},{18... | collective-permute-start | bytes 1572872 | tf_op jit(solution)/shard_map/ppermute | solution.py:22
  171.0 14.8 %collective-permute-start.5 = (f32[64,2,2,512]{3,0,2,1:T(8,128)}, f32[64,2,2,512]{3,0,2,1:T(8,128)}, u32[]{:S(2)}, u32[]{:S(2)}) collective-permute-start(f32[64,2,2,512]{3,0,2,1:T(8,128)} %copy.45), channel_id=1, source_target_pairs={{2,0},{4,2},{6,4},{8,6},{10,8},{12,10},{14,12},{16,14},{18,16},{20... | collective-permute-start | bytes 1572872 | tf_op jit(solution)/shard_map/ppermute | solution.py:25
  188.9 5.7 %collective-permute-start.6 = (f32[64,2,8,2]{0,3,2,1:T(2,128)S(1)}, f32[64,2,8,2]{0,3,2,1:T(2,128)S(1)}, u32[]{:S(2)}, u32[]{:S(2)}) collective-permute-start(f32[64,2,8,2]{0,3,2,1:T(2,128)S(1)} %get-tuple-element.9), channel_id=1, source_target_pairs={{0,1},{1,0},{2,3},{3,2},{4,5},{5,4},{6,7},{7,6},{8,9},{9,8},{10,11... | collective-permute-start | bytes 24584 | tf_op jit(solution)/shard_map/ppermute | solution.py:22
  190.5 4.1 %collective-permute-start.7 = (f32[64,2,8,2]{0,3,2,1:T(2,128)S(1)}, f32[64,2,8,2]{0,3,2,1:T(2,128)S(1)}, u32[]{:S(2)}, u32[]{:S(2)}) collective-permute-start(f32[64,2,8,2]{0,3,2,1:T(2,128)S(1)} %get-tuple-element.10), channel_id=1, source_target_pairs={{1,0},{0,1},{3,2},{2,3},{5,4},{4,5},{7,6},{6,7},{9,8},{8,9},{11,10... | collective-permute-start | bytes 24584 | tf_op jit(solution)/shard_map/ppermute | solution.py:25
  194.6 1.8 copy-start
  196.4 2.3 copy-start.5
  198.7 1.2 copy-start.4
  244.2 1.9 copy-start.2
